TPU v7x, 32 devices: a whole 2x2x4 slice. The times are simulated.
32 devices in a mesh: row: 8 (over z, x), col: 4 (over y, core).
Axes of the slice: x: 2, y: 2, z: 4, core: 2. Of those that a mesh axis runs over, the one named last changes fastest.
Arguments:
- tokens: bfloat16 [64, 512, 512], P('row', 'col'), may hold values from -6 to 6
- ln1_gain: float32 [512], replicated, may hold values from 0.1 to 1.9
- w_qkv: bfloat16 [512, 1536], replicated
- rel_bias: float32 [16, 49], replicated, may hold values from -4 to 4
- w_proj: bfloat16 [512, 512], replicated, may hold values from -0.25 to 0.25
- ln2_gain: float32 [512], replicated, may hold values from 0.1 to 1.9
- w_up: bfloat16 [512, 2048], replicated, may hold values from -0.25 to 0.25
- w_down: bfloat16 [2048, 512], replicated, may hold values from -0.125 to 0.125
- merge_gain: float32 [2048], replicated, may hold values from 0.3 to 3
- w_merge: bfloat16 [2048, 1024], replicated, may hold values from -0.125 to 0.125
- cotangent: bfloat16 [32, 256, 1024], P('row', 'col'), may hold values from -6 to 6
Outputs:
- merged: bfloat16 [32, 256, 1024], P('row', 'col')
- grad_merge: float32 [2048, 1024], P(('row', 'col'))
- grad_down: float32 [2048, 512], P(('row', 'col'))
All inputs are finite; a program needn't handle non-finite values.
Results may differ from a plain program's by a relative error of at most 0.012.
Values may be sent and summed in bfloat16 or wider, within the bound.
A program may use at most 128 MiB of HBM per device.

v0:
```python
import jax
import jax.numpy as jnp
from jax import lax
from jax.sharding import PartitionSpec as P


def with_halo(cells, sides, width):
    for axis, dim in sides:
        count = lax.axis_size(axis)
        ends = count - 1
        head = lax.slice_in_dim(cells, 0, width, axis=dim)
        tail = lax.slice_in_dim(cells, cells.shape[dim] - width, cells.shape[dim], axis=dim)
        cells = jnp.concatenate(
            [
                lax.ppermute(tail, axis, [(i, (i + 1) % count) for i in range(ends)]),
                cells,
                lax.ppermute(head, axis, [((i + 1) % count, i) for i in range(ends)]),
            ],
            axis=dim,
        )
    return cells


def layer_norm(value, gain):
    mean = jnp.mean(value, axis=-1, keepdims=True)
    var = jnp.mean((value - mean) ** 2, axis=-1, keepdims=True)
    return (value - mean) / jnp.sqrt(var + 1e-05) * gain


def local(
    tokens,
    ln1_gain,
    w_qkv,
    rel_bias,
    w_proj,
    ln2_gain,
    w_up,
    w_down,
    merge_gain,
    w_merge,
    cotangent,
):
    rows, cols, width = tokens.shape
    heads = rel_bias.shape[0]
    head_dim = width // heads
    x_flat = tokens.astype(jnp.float32).reshape(-1, width)
    normed = layer_norm(x_flat, ln1_gain).astype(jnp.bfloat16)
    query = jnp.dot(normed, w_qkv[:, :width], preferred_element_type=jnp.float32).astype(
        jnp.bfloat16
    )
    query_t = query.reshape(rows, cols, heads, head_dim).transpose(0, 2, 3, 1)
    keyval = jnp.dot(normed, w_qkv[:, width:], preferred_element_type=jnp.float32).astype(
        jnp.bfloat16
    )
    keyval = keyval.reshape(rows, cols, 2 * width).transpose(0, 2, 1)
    padded = with_halo(keyval, (("row", 0), ("col", 2)), 3)
    padded = padded.reshape(rows + 6, 2, heads, head_dim, cols + 6)
    total_rows = rows * lax.axis_size("row")
    total_cols = cols * lax.axis_size("col")
    row_pos = lax.axis_index("row") * rows + jnp.arange(rows)
    col_pos = lax.axis_index("col") * cols + jnp.arange(cols)
    scores = []
    masks = []
    for di in range(7):
        for dj in range(7):
            key = padded[di : di + rows, 0, :, :, dj : dj + cols]
            scores.append(
                jnp.einsum("rhdc,rhdc->rhc", query_t, key, preferred_element_type=jnp.float32)
            )
            rows_ok = (row_pos + di - 3 >= 0) & (row_pos + di - 3 < total_rows)
            cols_ok = (col_pos + dj - 3 >= 0) & (col_pos + dj - 3 < total_cols)
            masks.append(rows_ok[:, None] & cols_ok[None, :])
    scale = 1.0 / jnp.sqrt(jnp.float32(head_dim))
    score = jnp.stack(scores, 0) * scale + rel_bias.T[:, None, :, None]
    valid = jnp.stack(masks, 0)[:, :, None, :]
    score = jnp.where(valid, score, -1e30)
    top = jnp.max(score, axis=0, keepdims=True)
    expo = jnp.where(valid, jnp.exp(score - top), 0.0)
    probs = (expo / jnp.sum(expo, axis=0, keepdims=True)).astype(jnp.bfloat16)
    attn = jnp.zeros((rows, heads, head_dim, cols), jnp.float32)
    offset = 0
    for di in range(7):
        for dj in range(7):
            value = padded[di : di + rows, 1, :, :, dj : dj + cols]
            attn = attn + jnp.einsum(
                "rhc,rhdc->rhdc", probs[offset], value, preferred_element_type=jnp.float32
            )
            offset += 1
    attn = attn.astype(jnp.bfloat16).transpose(0, 3, 1, 2).reshape(-1, width)
    h_one = (x_flat + jnp.dot(attn, w_proj, preferred_element_type=jnp.float32)).astype(
        jnp.bfloat16
    )
    normed2 = layer_norm(h_one.astype(jnp.float32), ln2_gain).astype(jnp.bfloat16)
    hidden = jax.nn.gelu(
        jnp.dot(normed2, w_up, preferred_element_type=jnp.float32), approximate=False
    ).astype(jnp.bfloat16)
    out_y = (
        h_one.astype(jnp.float32) + jnp.dot(hidden, w_down, preferred_element_type=jnp.float32)
    ).astype(jnp.bfloat16)
    joined = (
        out_y.reshape(rows // 2, 2, cols // 2, 2, width)
        .transpose(0, 2, 3, 1, 4)
        .reshape(-1, 4 * width)
        .astype(jnp.float32)
    )
    mean = jnp.mean(joined, axis=-1, keepdims=True)
    inv = 1.0 / jnp.sqrt(jnp.mean((joined - mean) ** 2, axis=-1, keepdims=True) + 1e-05)
    unit = (joined - mean) * inv
    merge_in = (unit * merge_gain).astype(jnp.bfloat16)
    merged = jnp.dot(merge_in, w_merge, preferred_element_type=jnp.float32).astype(jnp.bfloat16)
    merged = merged.reshape(rows // 2, cols // 2, 2 * width)
    cot = cotangent.reshape(-1, 2 * width)
    grad_m = jnp.dot(merge_in.T, cot, preferred_element_type=jnp.float32)
    grad_n = jnp.dot(cot, w_merge.T, preferred_element_type=jnp.float32) * merge_gain
    grad_z = (
        grad_n
        - jnp.mean(grad_n, axis=-1, keepdims=True)
        - unit * jnp.mean(grad_n * unit, axis=-1, keepdims=True)
    ) * inv
    grad_y = (
        grad_z.astype(jnp.bfloat16)
        .reshape(rows // 2, cols // 2, 2, 2, width)
        .transpose(0, 3, 1, 2, 4)
        .reshape(-1, width)
    )
    grad_d = jnp.dot(hidden.T, grad_y, preferred_element_type=jnp.float32)
    count = grad_m.size + grad_d.size
    sum_m, sum_d = lax.psum((grad_m, grad_d), ("row", "col"))
    total = jnp.sum(sum_m * sum_m) + jnp.sum(sum_d * sum_d)
    groups = lax.axis_size(("row", "col"))
    index = lax.axis_index(("row", "col"))
    share_m = lax.dynamic_slice_in_dim(
        sum_m, index * (sum_m.shape[0] // groups), sum_m.shape[0] // groups, 0
    )
    share_d = lax.dynamic_slice_in_dim(
        sum_d, index * (sum_d.shape[0] // groups), sum_d.shape[0] // groups, 0
    )
    factor = 1.0 / jnp.sqrt(total / count + 1e-06)
    return (merged, share_m * factor, share_d * factor)


def solution(mesh):
    placed = (
        P("row", "col", None),
        P(),
        P(),
        P(),
        P(),
        P(),
        P(),
        P(),
        P(),
        P(),
        P("row", "col", None),
    )
    return jax.shard_map(
        local,
        mesh=mesh,
        in_specs=placed,
        out_specs=(P("row", "col", None), P(("row", "col"), None), P(("row", "col"), None)),
        check_vma=False,
    )
```

profile of v0, /device:TPU:0, one launch (start us, length us, event | category | flops | bytes accessed | tf_op | source)
XLA Modules:
  0.0 520.5 jit_solution(10870981523958563618)
XLA Ops:
  7.3 1.6 convert_reduce_fusion.1
  8.9 1.7 fusion.116
  11.1 2.6 convolution_convert_fusion
  13.7 3.9 copy.119
  17.6 2.6 fusion.141
  20.2 5.8 %collective-permute-start = (bf16[3,1024,128]{2,1,0:T(8,128)(2,1)}, bf16[3,1024,128]{2,1,0:T(8,128)(2,1)}, u32[]{:S(2)}, u32[]{:S(2)}) collective-permute-start(bf16[3,1024,128]{2,1,0:T(8,128)(2,1)} %get-tuple-element.58), channel_id=1, source_target_pairs={{0,4},{4,8},{8,12},{12,16},{16,20},{20,24},{24,28},{1,5},{5,9},{9,... | collective-permute-start | bytes 2359304 | tf_op jit(solution)/shard_map/ppermute | solution.py:15
  27.4 3.1 convolution_convert_fusion.1
  34.1 2.3 copy.118
  36.4 1.5 copy.518
  38.1 1.6 bitcast_convert_fusion
  39.6 19.4 %collective-permute-done = bf16[3,1024,128]{2,1,0:T(8,128)(2,1)} collective-permute-done((bf16[3,1024,128]{2,1,0:T(8,128)(2,1)}, bf16[3,1024,128]{2,1,0:T(8,128)(2,1)}, u32[]{:S(2)}, u32[]{:S(2)}) %collective-permute-start) | collective-permute-done | bytes 786464 | tf_op jit(solution)/shard_map/ppermute | solution.py:15
  59.0 1.6 pad_maximum_fusion.1
  60.6 4.3 fusion.140
  64.9 3.7 copy.120
  68.6 3.7 copy.121
  73.6 3.8 collective-permute-start.2
  78.2 3.9 copy.122
  82.1 3.1 copy.123
  85.2 8.4 %pad_maximum_fusion = bf16[14,1024,134]{2,1,0:T(8,128)(2,1)S(1)} fusion(bf16[14,1024,3]{2,1,0:T(8,128)(2,1)} %copy.123, bf16[3,1024,128]{2,1,0:T(8,128)(2,1)} %collective-permute-done.1, bf16[8,1024,128]{2,1,0:T(8,128)(2,1)} %bitcast.1631, bf16[3,1024,128]{2,1,0:T(8,128)(2,1)} %collective-permute-done, bf16[14,1024,3]{2,1,0:T(8,128)(2,1)} %copy.122), kind=kLoop, calls=%fused_computation.20 | loop fusion | flops 19210240 | bytes 7684096 | tf_op jit(solution)/shard_map/concatenate | solution.py:13
  93.6 7.9 %multiply_reduce_fusion.38 = (f32[8,16,128]{2,1,0:T(8,128)}, f32[8,16,128]{2,1,0:T(8,128)}, f32[8,16,128]{2,1,0:T(8,128)}, f32[8,16,128]{2,1,0:T(8,128)}, f32[8,...) fusion(bf16[14,2,16,32,134]{4,3,2,1,0:T(8,128)(2,1)S(1)} %bitca, ...), kind=kLoop, calls=%fused_computation.230 | loop fusion | flops 20234240 | bytes 16580608 | tf_op jit(solution)/shard_map/rhdc,rhdc->rhc/dot_general | solution.py:68
  101.5 12.3 %multiply_reduce_fusion.20 = (f32[8,16,128]{2,1,0:T(8,128)}, f32[8,16,128]{2,1,0:T(8,128)}, f32[8,16,128]{2,1,0:T(8,128)}, f32[8,16,128]{2,1,0:T(8,128)}, f32[8,...) fusion(bf16[14,2,16,32,134]{4,3,2,1,0:T(8,128)(2,1)S(1)} %bitca, ...), kind=kLoop, calls=%fused_computation.212 | loop fusion | flops 28016640 | bytes 22151168 | tf_op jit(solution)/shard_map/rhdc,rhdc->rhc/dot_general | solution.py:68
  113.8 11.8 %multiply_reduce_fusion.2 = (f32[8,16,128]{2,1,0:T(8,128)S(1)}, f32[8,16,128]{2,1,0:T(8,128)S(1)}, f32[8,16,128]{2,1,0:T(8,128)S(1)}, f32[8,16,128]{2,1,0:T(8,12...) fusion(bf16[14,2,16,32,134]{4,3,2,1,0:T(8,128)(2,1)S(1)} %bitca, ...), kind=kLoop, calls=%fused_computation.194 | loop fusion | flops 28016640 | bytes 22151168 | tf_op jit(solution)/shard_map/rhdc,rhdc->rhc/dot_general | solution.py:68
  141.8 1.3 divide_convert_fusion
  146.0 43.3 %fusion.19 = bf16[8,128,16,32]{1,3,2,0:T(8,128)(2,1)} fusion(bf16[14,2,16,32,134]{4,3,2,1,0:T(8,128)(2,1)} %bitcast.1629, f32[8,128,16]{1,2,0:T(8,128)} %get-tuple-element.61, f32[8,128,16]{1,2,0:T(8,128)} %get-tuple-element.62, f32[8,128,16]{1,2,0:T(8,128)} %get-tuple-element.63, f32[8,128,16]{1,2,0:T(8,128)} %get-tuple-element.64, ...), kind=kLoop, calls=%fused_computation.40 | loop fusion | flops 77070336 | bytes 55640064 | tf_op jit(solution)/shard_map/convert_element_type | solution.py:89
  189.3 2.0 copy.173
  192.7 20.9 %fusion.2 = bf16[1024,2048]{1,0:T(8,128)(2,1)S(1)} fusion(bf16[512,2048]{1,0:T(8,128)(2,1)S(1)} %copy-done, bf16[1024,512]{1,0:T(8,128)(2,1)S(1)} %get-tuple-element.112, f32[512]{0:T(512)S(1)} %copy-done.35, f32[1024]{0:T(1024)S(1)} %add_sqrt_fusion, f32[1024]{0:T(1024)S(1)} %broadcast_multiply_fusion), kind=kOutput, calls=%fused_computation.3 | convolution fusion | flops 2286419968 | bytes 7350272 | tf_op jit(solution)/shard_map/dot_general | solution.py:95
  213.6 1.9 copy-done.36
  215.5 3.7 fusion.122
  219.1 2.5 reshape.2795
  221.6 1.8 fusion.138
  223.5 4.1 multiply_reduce_fusion.52
  227.7 2.9 copy.583
  230.7 2.6 multiply_convert_fusion.1
  233.3 3.1 reshape.2695
  236.4 1.8 convert_element_type.87
  238.3 3.9 fusion.139
  242.2 1.7 multiply_convert_fusion
  244.0 2.6 reshape.2693
  246.6 3.0 copy.584
  249.6 2.5 reshape.2694
  252.1 6.8 %fusion.143 = f32[2048,512]{1,0:T(8,128)} fusion(bf16[1024,2048]{1,0:T(8,128)(2,1)} %copy-done.36, bf16[1024,512]{1,0:T(8,128)(2,1)} %reshape.2694), kind=kOutput, calls=%fused_computation.594 | convolution fusion | flops 2147483648 | bytes 9437184 | tf_op jit(solution)/shard_map/dot_general | solution.py:126
  259.0 4.5 fusion.142
  263.5 4.3 convolution_convert_fusion.2
  267.8 230.9 %all-reduce.3.cloned.1.call-done = (f32[2048,1024]{1,0:T(8,128)}, f32[2048,512]{1,0:T(8,128)}) async-done(((f32[2048,1024]{1,0:T(8,128)}, f32[2048,512]{1,0:T(8,128)}), (f32[2048,1024]{1,0:T(8,128)}, f32[2048,512]{1,0:T(8,128)})) %all-reduce.3.cloned.1.call-update) | async-done | bytes 12582928 | tf_op jit(solution)/shard_map/psum | solution.py:128
  498.7 3.9 multiply_reduce_fusion.1
  502.6 6.3 %multiply_reduce_fusion = f32[]{:T(128)} fusion(f32[2048,1024]{1,0:T(8,128)} %get-tuple-element.54), kind=kLoop, calls=%fused_computation.4 | loop fusion | flops 4194303 | bytes 8388612 | tf_op jit(solution)/shard_map/reduce_sum | solution.py:129
  510.2 1.7 dynamic-slice_multiply_fusion
  511.9 1.6 dynamic-slice_multiply_fusion.1
  (206 shorter events, 27.9 us)
Async XLA Ops:
  7.2 185.5 %copy-start = (bf16[512,2048]{1,0:T(8,128)(2,1)S(1)}, bf16[512,2048]{1,0:T(8,128)(2,1)}, u32[]{:S(2)}) copy-start(bf16[512,2048]{1,0:T(8,128)(2,1)} %param.17) | copy-start | bytes 6291460
  7.2 3.4 copy-start.5
  7.2 3.4 copy-start.31
  7.2 491.5 %all-reduce.3.cloned.1.call-start = ((), (), s32[]{:S(2)}) async-start(), calls=%async_computation | async-start | bytes 25165824 | tf_op jit(solution)/shard_map/psum | solution.py:128
  7.2 3.8 copy-start.33
  11.0 2.6 copy-start.7
  20.2 38.8 %collective-permute-start = (bf16[3,1024,128]{2,1,0:T(8,128)(2,1)}, bf16[3,1024,128]{2,1,0:T(8,128)(2,1)}, u32[]{:S(2)}, u32[]{:S(2)}) collective-permute-start(bf16[3,1024,128]{2,1,0:T(8,128)(2,1)} %get-tuple-element.58), channel_id=1, source_target_pairs={{0,4},{4,8},{8,12},{12,16},{16,20},{20,24},{24,28},{1,5},{5,9},{9,... | collective-permute-start | bytes 2359304 | tf_op jit(solution)/shard_map/ppermute | solution.py:15
  26.0 33.1 %collective-permute-start.1 = (bf16[3,1024,128]{2,1,0:T(8,128)(2,1)}, bf16[3,1024,128]{2,1,0:T(8,128)(2,1)}, u32[]{:S(2)}, u32[]{:S(2)}) collective-permute-start(bf16[3,1024,128]{2,1,0:T(8,128)(2,1)} %get-tuple-element.59), channel_id=1, source_target_pairs={{4,0},{8,4},{12,8},{16,12},{20,16},{24,20},{28,24},{5,1},{9,5},{13... | collective-permute-start | bytes 2359304 | tf_op jit(solution)/shard_map/ppermute | solution.py:17
  37.9 21.1 %copy-start.4 = (bf16[8,128,1024]{1,2,0:T(8,128)(2,1)S(1)}, bf16[8,128,1024]{1,2,0:T(8,128)(2,1)}, u32[]{:S(2)}) copy-start(bf16[8,128,1024]{1,2,0:T(8,128)(2,1)} %copy.119) | copy-start | bytes 6291460
  68.6 8.9 %copy-start.27 = (f32[2048]{0:T(1024)S(1)}, f32[2048]{0:T(1024)}, u32[]{:S(2)}) copy-start(f32[2048]{0:T(1024)} %param.19) | copy-start | bytes 24580
  68.6 9.5 %copy-start.30 = (f32[16,49]{1,0:T(8,128)S(1)}, f32[16,49]{1,0:T(8,128)}, u32[]{:S(2)}) copy-start(f32[16,49]{1,0:T(8,128)} %param.14) | copy-start | bytes 9412
  72.3 9.8 %collective-permute-start.3 = (bf16[14,1024,3]{1,0,2:T(8,128)(2,1)S(1)}, bf16[14,1024,3]{1,0,2:T(8,128)(2,1)S(1)}, u32[]{:S(2)}, u32[]{:S(2)}) collective-permute-start(bf16[14,1024,3]{1,0,2:T(8,128)(2,1)S(1)} %copy.121), channel_id=1, source_target_pairs={{1,0},{2,1},{3,2},{5,4},{6,5},{7,6},{9,8},{10,9},{11,10},{13,12},{... | collective-permute-start | bytes 258056 | tf_op jit(solution)/shard_map/ppermute | solution.py:17
  73.6 4.6 collective-permute-start.2
  85.2 8.4 %copy-start.3 = (f32[8,16,128,32]{2,0,3,1:T(8,128)S(1)}, f32[8,16,128,32]{2,0,3,1:T(8,128)}, u32[]{:S(2)}) copy-start(f32[8,16,128,32]{2,0,3,1:T(8,128)} %bitcast_convert_fusion) | copy-start | bytes 6291460
  93.6 20.2 %copy-start.2 = (bf16[14,1024,134]{2,1,0:T(8,128)(2,1)}, bf16[14,1024,134]{2,1,0:T(8,128)(2,1)S(1)}, u32[]{:S(2)}) copy-start(bf16[14,1024,134]{2,1,0:T(8,128)(2,1)S(1)} %pad_maximum_fusion) | copy-start | bytes 11526148
  125.6 13.9 %copy-start.26 = (f32[8,16,128]{2,1,0:T(8,128)S(1)}, f32[8,16,128]{2,1,0:T(8,128)}, u32[]{:S(2)}) copy-start(f32[8,16,128]{2,1,0:T(8,128)} %get-tuple-element.35) | copy-start | bytes 196612
  125.6 13.9 %copy-start.25 = (f32[8,16,128]{2,1,0:T(8,128)S(1)}, f32[8,16,128]{2,1,0:T(8,128)}, u32[]{:S(2)}) copy-start(f32[8,16,128]{2,1,0:T(8,128)} %get-tuple-element.34) | copy-start | bytes 196612
  125.6 13.9 %copy-start.24 = (f32[8,16,128]{2,1,0:T(8,128)S(1)}, f32[8,16,128]{2,1,0:T(8,128)}, u32[]{:S(2)}) copy-start(f32[8,16,128]{2,1,0:T(8,128)} %get-tuple-element.33) | copy-start | bytes 196612
  125.6 13.9 %copy-start.23 = (f32[8,16,128]{2,1,0:T(8,128)S(1)}, f32[8,16,128]{2,1,0:T(8,128)}, u32[]{:S(2)}) copy-start(f32[8,16,128]{2,1,0:T(8,128)} %get-tuple-element.32) | copy-start | bytes 196612
  125.6 14.0 %copy-start.22 = (f32[8,16,128]{2,1,0:T(8,128)S(1)}, f32[8,16,128]{2,1,0:T(8,128)}, u32[]{:S(2)}) copy-start(f32[8,16,128]{2,1,0:T(8,128)} %get-tuple-element.31) | copy-start | bytes 196612
  125.6 14.0 %copy-start.21 = (f32[8,16,128]{2,1,0:T(8,128)S(1)}, f32[8,16,128]{2,1,0:T(8,128)}, u32[]{:S(2)}) copy-start(f32[8,16,128]{2,1,0:T(8,128)} %get-tuple-element.30) | copy-start | bytes 196612
  125.6 14.0 %copy-start.20 = (f32[8,16,128]{2,1,0:T(8,128)S(1)}, f32[8,16,128]{2,1,0:T(8,128)}, u32[]{:S(2)}) copy-start(f32[8,16,128]{2,1,0:T(8,128)} %get-tuple-element.29) | copy-start | bytes 196612
  125.6 14.0 %copy-start.19 = (f32[8,16,128]{2,1,0:T(8,128)S(1)}, f32[8,16,128]{2,1,0:T(8,128)}, u32[]{:S(2)}) copy-start(f32[8,16,128]{2,1,0:T(8,128)} %get-tuple-element.28) | copy-start | bytes 196612
  125.6 14.0 %copy-start.18 = (f32[8,16,128]{2,1,0:T(8,128)S(1)}, f32[8,16,128]{2,1,0:T(8,128)}, u32[]{:S(2)}) copy-start(f32[8,16,128]{2,1,0:T(8,128)} %get-tuple-element.27) | copy-start | bytes 196612
  125.6 14.0 %copy-start.17 = (f32[8,16,128]{2,1,0:T(8,128)S(1)}, f32[8,16,128]{2,1,0:T(8,128)}, u32[]{:S(2)}) copy-start(f32[8,16,128]{2,1,0:T(8,128)} %get-tuple-element.26) | copy-start | bytes 196612
  125.6 14.0 %copy-start.16 = (f32[8,16,128]{2,1,0:T(8,128)S(1)}, f32[8,16,128]{2,1,0:T(8,128)}, u32[]{:S(2)}) copy-start(f32[8,16,128]{2,1,0:T(8,128)} %get-tuple-element.25) | copy-start | bytes 196612
  125.7 14.1 %copy-start.15 = (f32[8,16,128]{2,1,0:T(8,128)S(1)}, f32[8,16,128]{2,1,0:T(8,128)}, u32[]{:S(2)}) copy-start(f32[8,16,128]{2,1,0:T(8,128)} %get-tuple-element.24) | copy-start | bytes 196612
  125.7 14.1 %copy-start.14 = (f32[8,16,128]{2,1,0:T(8,128)S(1)}, f32[8,16,128]{2,1,0:T(8,128)}, u32[]{:S(2)}) copy-start(f32[8,16,128]{2,1,0:T(8,128)} %get-tuple-element.23) | copy-start | bytes 196612
  125.7 14.1 %copy-start.13 = (f32[8,16,128]{2,1,0:T(8,128)S(1)}, f32[8,16,128]{2,1,0:T(8,128)}, u32[]{:S(2)}) copy-start(f32[8,16,128]{2,1,0:T(8,128)} %get-tuple-element.22) | copy-start | bytes 196612
  125.7 14.1 %copy-start.12 = (f32[8,16,128]{2,1,0:T(8,128)S(1)}, f32[8,16,128]{2,1,0:T(8,128)}, u32[]{:S(2)}) copy-start(f32[8,16,128]{2,1,0:T(8,128)} %get-tuple-element.21) | copy-start | bytes 196612
  125.7 14.1 %copy-start.11 = (f32[8,16,128]{2,1,0:T(8,128)S(1)}, f32[8,16,128]{2,1,0:T(8,128)}, u32[]{:S(2)}) copy-start(f32[8,16,128]{2,1,0:T(8,128)} %get-tuple-element.20) | copy-start | bytes 196612
  125.7 14.1 %copy-start.10 = (f32[8,16,128]{2,1,0:T(8,128)S(1)}, f32[8,16,128]{2,1,0:T(8,128)}, u32[]{:S(2)}) copy-start(f32[8,16,128]{2,1,0:T(8,128)} %get-tuple-element.19) | copy-start | bytes 196612
  126.7 13.1 %copy-start.9 = (f32[8,16,128]{2,1,0:T(8,128)S(1)}, f32[8,16,128]{2,1,0:T(8,128)}, u32[]{:S(2)}) copy-start(f32[8,16,128]{2,1,0:T(8,128)} %get-tuple-element.18) | copy-start | bytes 196612
  127.6 12.3 %copy-start.8 = (f32[8,16,128]{2,1,0:T(8,128)S(1)}, f32[8,16,128]{2,1,0:T(8,128)}, u32[]{:S(2)}) copy-start(f32[8,16,128]{2,1,0:T(8,128)} %get-tuple-element.17) | copy-start | bytes 196612
  189.2 2.0 copy-start.34
  191.2 1.4 copy-start.35
  192.6 22.8 %copy-start.32 = (bf16[2048,512]{1,0:T(8,128)(2,1)S(1)}, bf16[2048,512]{1,0:T(8,128)(2,1)}, u32[]{:S(2)}) copy-start(bf16[2048,512]{1,0:T(8,128)(2,1)} %param.18) | copy-start | bytes 6291460
  213.5 1.9 copy-start.36
  227.6 3.1 copy-start.29
  236.4 1.9 copy-start.28
  252.1 6.9 %copy-start.6 = (bf16[4,64,1024]{2,1,0:T(8,128)(2,1)S(1)}, bf16[4,64,1024]{2,1,0:T(8,128)(2,1)}, u32[]{:S(2)}) copy-start(bf16[4,64,1024]{2,1,0:T(8,128)(2,1)} %param.21) | copy-start | bytes 1572868
  502.6 10.9 %copy-start.1 = (bf16[512,2048]{1,0:T(8,128)(2,1)S(1)}, bf16[512,2048]{1,0:T(8,128)(2,1)}, u32[]{:S(2)}) copy-start(bf16[512,2048]{1,0:T(8,128)(2,1)} %param.17) | copy-start | bytes 6291460
Sparse Core Ops, SparseCore 0:
  263.6 235.0 all-reduce.2
where the time goes:
time: 527 us; the launch traced here: 521 us
  waiting for transfers between devices  250 us (47%)
  other arithmetic  125 us (24%)
  local copies, waits for them, and re-layouts  66.3 us (13%)
  matrix products  50.6 us (10%)
  between operations  16.6 us (3%)
  starting transfers between devices  12.2 us (2%)
    psum x1, waiting for transfers between devices, local(): sum_m, sum_d = lax.psum((grad_m, grad_d), ('row', 'col'))  231 us
    convert_element_type x1, other arithmetic, local(): attn = attn.astype(jnp.bfloat16).transpose(0, 3, 1, 2).reshape(-1, width)  43.3 us
    dot_general x3, other arithmetic, local(): jnp.einsum('rhdc,rhdc->rhc', query_t, key, preferred_element_type=jnp.flo...  31.9 us
    dot_general x1, matrix products, local(): jnp.dot(normed2, w_up, preferred_element_type=jnp.float32)  20.9 us
    ppermute x2, waiting for transfers between devices, with_halo(): lax.ppermute(tail, axis, [(i, (i + 1) % count) for i in range(ends)])  19.4 us
    unnamed x123, local copies, waits for them, and re-layouts  17.5 us
    slice x3, local copies, waits for them, and re-layouts, with_halo(): lax.slice_in_dim(cells, cells.shape[dim] - width, cells.shape[dim], axis=...  10.6 us
  transfers between devices with their start and end apart: 5, of which 2 were waited for; matrix products, arithmetic and copies ran while one was open for 4% of the time, Pallas kernels for 0%

commit v1 on v0

--- a/solution.py
+++ b/solution.py
@@ -125,7 +125,7 @@
     )
     grad_d = jnp.dot(hidden.T, grad_y, preferred_element_type=jnp.float32)
     count = grad_m.size + grad_d.size
-    sum_m, sum_d = lax.psum((grad_m, grad_d), ("row", "col"))
+    sum_m, sum_d = lax.psum(lax.psum((grad_m, grad_d), "row"), "col")
     total = jnp.sum(sum_m * sum_m) + jnp.sum(sum_d * sum_d)
     groups = lax.axis_size(("row", "col"))
     index = lax.axis_index(("row", "col"))

time: 527 us -> 914 us (1.73)
  waiting for transfers between devices: 250 us -> 636 us
    psum x1 -> x2, waiting for transfers between devices: 231 us -> 617 us  [local(): sum_m, sum_d = lax.psum(lax.psum((grad_m, grad_d), 'row'), 'col')]
  transfers between devices with their start and end apart: 5 -> 6, of which waited for: 2 -> 3; matrix products, arithmetic and copies ran while one was open for 4% -> 2% of each run, Pallas kernels for 0% -> 0%
where the time goes in v1:
time: 914 us; the launch traced here: 907 us
  waiting for transfers between devices  636 us (70%)
  other arithmetic  125 us (14%)
  local copies, waits for them, and re-layouts  66.1 us (7%)
  matrix products  50.6 us (6%)
  between operations  16.6 us (2%)
  starting transfers between devices  12.5 us (1%)
    psum x2, waiting for transfers between devices, local(): sum_m, sum_d = lax.psum(lax.psum((grad_m, grad_d), 'row'), 'col')  617 us
    convert_element_type x1, other arithmetic, local(): attn = attn.astype(jnp.bfloat16).transpose(0, 3, 1, 2).reshape(-1, width)  43.3 us
    dot_general x3, other arithmetic, local(): jnp.einsum('rhdc,rhdc->rhc', query_t, key, preferred_element_type=jnp.flo...  31.9 us
    dot_general x1, matrix products, local(): jnp.dot(normed2, w_up, preferred_element_type=jnp.float32)  20.9 us
    ppermute x2, waiting for transfers between devices, with_halo(): lax.ppermute(tail, axis, [(i, (i + 1) % count) for i in range(ends)])  19.4 us
  transfers between devices with their start and end apart: 6, of which 3 were waited for; matrix products, arithmetic and copies ran while one was open for 2% of the time, Pallas kernels for 0%

profile of v1, /device:TPU:0, one launch (start us, length us, event | category | flops | bytes accessed | tf_op | source)
XLA Modules:
  0.0 906.7 jit_solution(2606089179599154916)
XLA Ops:
  7.3 1.6 convert_reduce_fusion.1
  8.9 1.7 fusion.116
  11.1 2.6 convolution_convert_fusion
  13.7 3.9 copy.119
  17.6 2.6 fusion.141
  20.2 5.8 collective-permute-start
  27.4 3.1 convolution_convert_fusion.1
  34.1 2.3 copy.118
  36.4 1.5 copy.518
  38.1 1.6 bitcast_convert_fusion
  39.6 19.4 %collective-permute-done = bf16[3,1024,128]{2,1,0:T(8,128)(2,1)} collective-permute-done((bf16[3,1024,128]{2,1,0:T(8,128)(2,1)}, bf16[3,1024,128]{2,1,0:T(8,128)(2,1)}, u32[]{:S(2)}, u32[]{:S(2)}) %collective-permute-start) | collective-permute-done | bytes 786464 | tf_op jit(solution)/shard_map/ppermute | solution.py:15
  59.0 1.6 pad_maximum_fusion.1
  60.6 4.3 fusion.140
  64.9 3.7 copy.120
  68.6 3.7 copy.121
  73.6 3.8 collective-permute-start.2
  78.2 3.9 copy.122
  82.1 3.1 copy.123
  85.2 8.4 pad_maximum_fusion
  93.6 7.9 multiply_reduce_fusion.38
  101.5 12.3 %multiply_reduce_fusion.20 = (f32[8,16,128]{2,1,0:T(8,128)}, f32[8,16,128]{2,1,0:T(8,128)}, f32[8,16,128]{2,1,0:T(8,128)}, f32[8,16,128]{2,1,0:T(8,128)}, f32[8,...) fusion(bf16[14,2,16,32,134]{4,3,2,1,0:T(8,128)(2,1)S(1)} %bitca, ...), kind=kLoop, calls=%fused_computation.212 | loop fusion | flops 28016640 | bytes 22151168 | tf_op jit(solution)/shard_map/rhdc,rhdc->rhc/dot_general | solution.py:68
  113.8 11.8 %multiply_reduce_fusion.2 = (f32[8,16,128]{2,1,0:T(8,128)S(1)}, f32[8,16,128]{2,1,0:T(8,128)S(1)}, f32[8,16,128]{2,1,0:T(8,128)S(1)}, f32[8,16,128]{2,1,0:T(8,12...) fusion(bf16[14,2,16,32,134]{4,3,2,1,0:T(8,128)(2,1)S(1)} %bitca, ...), kind=kLoop, calls=%fused_computation.194 | loop fusion | flops 28016640 | bytes 22151168 | tf_op jit(solution)/shard_map/rhdc,rhdc->rhc/dot_general | solution.py:68
  146.0 43.3 %fusion.19 = bf16[8,128,16,32]{1,3,2,0:T(8,128)(2,1)} fusion(bf16[14,2,16,32,134]{4,3,2,1,0:T(8,128)(2,1)} %bitcast.1629, f32[8,128,16]{1,2,0:T(8,128)} %get-tuple-element.63, f32[8,128,16]{1,2,0:T(8,128)} %get-tuple-element.64, f32[8,128,16]{1,2,0:T(8,128)} %get-tuple-element.65, f32[8,128,16]{1,2,0:T(8,128)} %get-tuple-element.66, ...), kind=kLoop, calls=%fused_computation.40 | loop fusion | flops 77070336 | bytes 55640064 | tf_op jit(solution)/shard_map/convert_element_type | solution.py:89
  189.3 2.0 copy.173
  192.7 20.9 %fusion.2 = bf16[1024,2048]{1,0:T(8,128)(2,1)S(1)} fusion(bf16[512,2048]{1,0:T(8,128)(2,1)S(1)} %copy-done, bf16[1024,512]{1,0:T(8,128)(2,1)S(1)} %get-tuple-element.114, f32[512]{0:T(512)S(1)} %copy-done.35, f32[1024]{0:T(1024)S(1)} %add_sqrt_fusion, f32[1024]{0:T(1024)S(1)} %broadcast_multiply_fusion), kind=kOutput, calls=%fused_computation.3 | convolution fusion | flops 2286419968 | bytes 7350272 | tf_op jit(solution)/shard_map/dot_general | solution.py:95
  213.6 1.9 copy-done.36
  215.5 3.7 fusion.122
  219.1 2.5 reshape.2795
  221.6 1.8 fusion.138
  223.5 4.1 multiply_reduce_fusion.52
  227.7 2.9 copy.583
  230.7 2.6 multiply_convert_fusion.1
  233.3 3.1 reshape.2695
  236.4 1.8 convert_element_type.87
  238.3 3.9 fusion.139
  242.2 1.7 multiply_convert_fusion
  244.0 2.6 reshape.2693
  246.6 3.0 copy.584
  249.6 2.3 reshape.2694
  251.9 6.9 fusion.143
  258.8 4.5 fusion.142
  263.6 398.8 %all-reduce.5.cloned.1.call-done = (f32[2048,1024]{1,0:T(8,128)}, f32[2048,512]{1,0:T(8,128)}) async-done(((f32[2048,1024]{1,0:T(8,128)}, f32[2048,512]{1,0:T(8,128)}), (f32[2048,1024]{1,0:T(8,128)}, f32[2048,512]{1,0:T(8,128)})) %all-reduce.5.cloned.1.call-update) | async-done | bytes 12582928 | tf_op jit(solution)/shard_map/psum | solution.py:128
  662.4 4.3 convolution_convert_fusion.2
  666.7 218.2 %all-reduce.7.cloned.1.call-done = (f32[2048,1024]{1,0:T(8,128)}, f32[2048,512]{1,0:T(8,128)}) async-done(((f32[2048,1024]{1,0:T(8,128)}, f32[2048,512]{1,0:T(8,128)}), (f32[2048,1024]{1,0:T(8,128)}, f32[2048,512]{1,0:T(8,128)})) %all-reduce.7.cloned.1.call-update) | async-done | bytes 12582928 | tf_op jit(solution)/shard_map/psum | solution.py:128
  884.8 3.9 multiply_reduce_fusion.1
  888.7 6.3 multiply_reduce_fusion
  896.3 1.7 dynamic-slice_multiply_fusion
  898.0 1.6 dynamic-slice_multiply_fusion.1
  (209 shorter events, 29.5 us)
Async XLA Ops:
  7.2 185.5 %copy-start = (bf16[512,2048]{1,0:T(8,128)(2,1)S(1)}, bf16[512,2048]{1,0:T(8,128)(2,1)}, u32[]{:S(2)}) copy-start(bf16[512,2048]{1,0:T(8,128)(2,1)} %param.17) | copy-start | bytes 6291460
  7.2 3.4 copy-start.5
  7.2 3.4 copy-start.31
  7.2 655.1 %all-reduce.5.cloned.1.call-start = ((), (), s32[]{:S(2)}) async-start(), calls=%async_computation | async-start | bytes 25165824 | tf_op jit(solution)/shard_map/psum | solution.py:128
  7.2 3.8 copy-start.33
  11.0 2.6 copy-start.7
  20.2 38.8 %collective-permute-start = (bf16[3,1024,128]{2,1,0:T(8,128)(2,1)}, bf16[3,1024,128]{2,1,0:T(8,128)(2,1)}, u32[]{:S(2)}, u32[]{:S(2)}) collective-permute-start(bf16[3,1024,128]{2,1,0:T(8,128)(2,1)} %get-tuple-element.60), channel_id=1, source_target_pairs={{0,4},{4,8},{8,12},{12,16},{16,20},{20,24},{24,28},{1,5},{5,9},{9,... | collective-permute-start | bytes 2359304 | tf_op jit(solution)/shard_map/ppermute | solution.py:15
  26.0 33.1 %collective-permute-start.1 = (bf16[3,1024,128]{2,1,0:T(8,128)(2,1)}, bf16[3,1024,128]{2,1,0:T(8,128)(2,1)}, u32[]{:S(2)}, u32[]{:S(2)}) collective-permute-start(bf16[3,1024,128]{2,1,0:T(8,128)(2,1)} %get-tuple-element.61), channel_id=1, source_target_pairs={{4,0},{8,4},{12,8},{16,12},{20,16},{24,20},{28,24},{5,1},{9,5},{13... | collective-permute-start | bytes 2359304 | tf_op jit(solution)/shard_map/ppermute | solution.py:17
  37.9 21.1 %copy-start.4 = (bf16[8,128,1024]{1,2,0:T(8,128)(2,1)S(1)}, bf16[8,128,1024]{1,2,0:T(8,128)(2,1)}, u32[]{:S(2)}) copy-start(bf16[8,128,1024]{1,2,0:T(8,128)(2,1)} %copy.119) | copy-start | bytes 6291460
  68.6 8.9 copy-start.27
  68.6 9.5 %copy-start.30 = (f32[16,49]{1,0:T(8,128)S(1)}, f32[16,49]{1,0:T(8,128)}, u32[]{:S(2)}) copy-start(f32[16,49]{1,0:T(8,128)} %param.14) | copy-start | bytes 9412
  72.3 9.8 %collective-permute-start.3 = (bf16[14,1024,3]{1,0,2:T(8,128)(2,1)S(1)}, bf16[14,1024,3]{1,0,2:T(8,128)(2,1)S(1)}, u32[]{:S(2)}, u32[]{:S(2)}) collective-permute-start(bf16[14,1024,3]{1,0,2:T(8,128)(2,1)S(1)} %copy.121), channel_id=1, source_target_pairs={{1,0},{2,1},{3,2},{5,4},{6,5},{7,6},{9,8},{10,9},{11,10},{13,12},{... | collective-permute-start | bytes 258056 | tf_op jit(solution)/shard_map/ppermute | solution.py:17
  73.6 4.6 collective-permute-start.2
  85.2 8.4 copy-start.3
  93.6 20.2 %copy-start.2 = (bf16[14,1024,134]{2,1,0:T(8,128)(2,1)}, bf16[14,1024,134]{2,1,0:T(8,128)(2,1)S(1)}, u32[]{:S(2)}) copy-start(bf16[14,1024,134]{2,1,0:T(8,128)(2,1)S(1)} %pad_maximum_fusion) | copy-start | bytes 11526148
  125.6 13.9 %copy-start.26 = (f32[8,16,128]{2,1,0:T(8,128)S(1)}, f32[8,16,128]{2,1,0:T(8,128)}, u32[]{:S(2)}) copy-start(f32[8,16,128]{2,1,0:T(8,128)} %get-tuple-element.35) | copy-start | bytes 196612
  125.6 13.9 %copy-start.25 = (f32[8,16,128]{2,1,0:T(8,128)S(1)}, f32[8,16,128]{2,1,0:T(8,128)}, u32[]{:S(2)}) copy-start(f32[8,16,128]{2,1,0:T(8,128)} %get-tuple-element.34) | copy-start | bytes 196612
  125.6 13.9 %copy-start.24 = (f32[8,16,128]{2,1,0:T(8,128)S(1)}, f32[8,16,128]{2,1,0:T(8,128)}, u32[]{:S(2)}) copy-start(f32[8,16,128]{2,1,0:T(8,128)} %get-tuple-element.33) | copy-start | bytes 196612
  125.6 13.9 %copy-start.23 = (f32[8,16,128]{2,1,0:T(8,128)S(1)}, f32[8,16,128]{2,1,0:T(8,128)}, u32[]{:S(2)}) copy-start(f32[8,16,128]{2,1,0:T(8,128)} %get-tuple-element.32) | copy-start | bytes 196612
  125.6 14.0 %copy-start.22 = (f32[8,16,128]{2,1,0:T(8,128)S(1)}, f32[8,16,128]{2,1,0:T(8,128)}, u32[]{:S(2)}) copy-start(f32[8,16,128]{2,1,0:T(8,128)} %get-tuple-element.31) | copy-start | bytes 196612
  125.6 14.0 %copy-start.21 = (f32[8,16,128]{2,1,0:T(8,128)S(1)}, f32[8,16,128]{2,1,0:T(8,128)}, u32[]{:S(2)}) copy-start(f32[8,16,128]{2,1,0:T(8,128)} %get-tuple-element.30) | copy-start | bytes 196612
  125.6 14.0 %copy-start.20 = (f32[8,16,128]{2,1,0:T(8,128)S(1)}, f32[8,16,128]{2,1,0:T(8,128)}, u32[]{:S(2)}) copy-start(f32[8,16,128]{2,1,0:T(8,128)} %get-tuple-element.29) | copy-start | bytes 196612
  125.6 14.0 %copy-start.19 = (f32[8,16,128]{2,1,0:T(8,128)S(1)}, f32[8,16,128]{2,1,0:T(8,128)}, u32[]{:S(2)}) copy-start(f32[8,16,128]{2,1,0:T(8,128)} %get-tuple-element.28) | copy-start | bytes 196612
  125.6 14.0 %copy-start.18 = (f32[8,16,128]{2,1,0:T(8,128)S(1)}, f32[8,16,128]{2,1,0:T(8,128)}, u32[]{:S(2)}) copy-start(f32[8,16,128]{2,1,0:T(8,128)} %get-tuple-element.27) | copy-start | bytes 196612
  125.6 14.0 %copy-start.17 = (f32[8,16,128]{2,1,0:T(8,128)S(1)}, f32[8,16,128]{2,1,0:T(8,128)}, u32[]{:S(2)}) copy-start(f32[8,16,128]{2,1,0:T(8,128)} %get-tuple-element.26) | copy-start | bytes 196612
  125.6 14.0 %copy-start.16 = (f32[8,16,128]{2,1,0:T(8,128)S(1)}, f32[8,16,128]{2,1,0:T(8,128)}, u32[]{:S(2)}) copy-start(f32[8,16,128]{2,1,0:T(8,128)} %get-tuple-element.25) | copy-start | bytes 196612
  125.7 14.1 %copy-start.15 = (f32[8,16,128]{2,1,0:T(8,128)S(1)}, f32[8,16,128]{2,1,0:T(8,128)}, u32[]{:S(2)}) copy-start(f32[8,16,128]{2,1,0:T(8,128)} %get-tuple-element.24) | copy-start | bytes 196612
  125.7 14.1 %copy-start.14 = (f32[8,16,128]{2,1,0:T(8,128)S(1)}, f32[8,16,128]{2,1,0:T(8,128)}, u32[]{:S(2)}) copy-start(f32[8,16,128]{2,1,0:T(8,128)} %get-tuple-element.23) | copy-start | bytes 196612
  125.7 14.1 %copy-start.13 = (f32[8,16,128]{2,1,0:T(8,128)S(1)}, f32[8,16,128]{2,1,0:T(8,128)}, u32[]{:S(2)}) copy-start(f32[8,16,128]{2,1,0:T(8,128)} %get-tuple-element.22) | copy-start | bytes 196612
  125.7 14.1 %copy-start.12 = (f32[8,16,128]{2,1,0:T(8,128)S(1)}, f32[8,16,128]{2,1,0:T(8,128)}, u32[]{:S(2)}) copy-start(f32[8,16,128]{2,1,0:T(8,128)} %get-tuple-element.21) | copy-start | bytes 196612
  125.7 14.1 %copy-start.11 = (f32[8,16,128]{2,1,0:T(8,128)S(1)}, f32[8,16,128]{2,1,0:T(8,128)}, u32[]{:S(2)}) copy-start(f32[8,16,128]{2,1,0:T(8,128)} %get-tuple-element.20) | copy-start | bytes 196612
  125.7 14.1 %copy-start.10 = (f32[8,16,128]{2,1,0:T(8,128)S(1)}, f32[8,16,128]{2,1,0:T(8,128)}, u32[]{:S(2)}) copy-start(f32[8,16,128]{2,1,0:T(8,128)} %get-tuple-element.19) | copy-start | bytes 196612
  126.7 13.1 %copy-start.9 = (f32[8,16,128]{2,1,0:T(8,128)S(1)}, f32[8,16,128]{2,1,0:T(8,128)}, u32[]{:S(2)}) copy-start(f32[8,16,128]{2,1,0:T(8,128)} %get-tuple-element.18) | copy-start | bytes 196612
  127.6 12.3 %copy-start.8 = (f32[8,16,128]{2,1,0:T(8,128)S(1)}, f32[8,16,128]{2,1,0:T(8,128)}, u32[]{:S(2)}) copy-start(f32[8,16,128]{2,1,0:T(8,128)} %get-tuple-element.17) | copy-start | bytes 196612
  189.2 2.0 copy-start.34
  191.2 1.4 copy-start.35
  192.6 22.8 %copy-start.32 = (bf16[2048,512]{1,0:T(8,128)(2,1)S(1)}, bf16[2048,512]{1,0:T(8,128)(2,1)}, u32[]{:S(2)}) copy-start(bf16[2048,512]{1,0:T(8,128)(2,1)} %param.18) | copy-start | bytes 6291460
  213.5 1.9 copy-start.36
  227.6 3.1 copy-start.29
  236.4 1.9 copy-start.28
  251.9 6.9 copy-start.6
  263.3 621.5 %all-reduce.7.cloned.1.call-start = ((), (), s32[]{:S(2)}) async-start(), calls=%async_computation.1 | async-start | bytes 25165824 | tf_op jit(solution)/shard_map/psum | solution.py:128
  888.7 10.9 %copy-start.1 = (bf16[512,2048]{1,0:T(8,128)(2,1)S(1)}, bf16[512,2048]{1,0:T(8,128)(2,1)}, u32[]{:S(2)}) copy-start(bf16[512,2048]{1,0:T(8,128)(2,1)} %param.17) | copy-start | bytes 6291460
Sparse Core Ops, SparseCore 0:
  263.5 398.8 all-reduce.4
  665.0 219.7 all-reduce.6
